TPU v7x, 512 devices: a whole 4x4x16 slice. The times are simulated.
512 devices in a mesh: tile: 64 (over x, z_lo, core), agent: 8 (over z_hi, y).
Axes of the slice: x: 4, y: 4, z: 16 (z_hi: 2, z_lo: 8; z = z_hi * 8 + z_lo), core: 2. Of those that a mesh axis runs over, the one named last changes fastest.
Arguments:
- states: float32 [8, 8, 128, 256], P('agent', None, 'tile'), may hold values from -6 to 6
- footprints: float32 [64, 64, 64, 512], P('agent', 'tile'), may hold values from -0.25 to 0.25
- offsets: int32 [64, 64], P('agent', 'tile'), may hold values from 0 to 1984, as said below
- measured: float32 [64, 8, 2048], P('agent', None, 'tile'), may hold values from -9 to 9
- weights: float32 [64, 8, 2048], P('agent', None, 'tile'), may hold values from 0.2 to 5
Outputs:
- new_states: float32 [8, 8, 128, 256], P('agent', None, 'tile')
- prior_volume: float32 [8, 128, 256], P(None, 'tile')
Inputs may be any that keep to these rules, and one draw needn't show every extreme that they name: For one agent and one tile t, the values offsets[v, t] // 32 differ between the agent's 8 views v.
All inputs are finite; a program needn't handle non-finite values.
Results may differ from a plain program's by a relative error of at most 0.0003.
Values sent between devices are 32-bit elements; how exact they have to be, the bound alone decides.
No kernel may reach another device: no remote copies, remote signals or barrier semaphores. Data moves between devices by JAX's collectives and lax.ppermute only.
A program may use at most 64 MiB of HBM per device.

v0:
```python
import jax
import jax.numpy as jnp
from jax import lax
from jax.sharding import PartitionSpec as P

SWEEPS = 2
STEP_SIZE = 0.25
RELAX = 0.6
QRATIO = 0.6


def with_halo(value, sides, width):
    for axis, dim in sides:
        count, length = (lax.axis_size(axis), value.shape[dim])
        up = [(i, (i + 1) % count) for i in range(count - 1)]
        down = [(j, i) for i, j in up]
        last = lax.slice_in_dim(value, length - width, length, axis=dim)
        first = lax.slice_in_dim(value, 0, width, axis=dim)
        before = lax.ppermute(last, axis, up)
        after = lax.ppermute(first, axis, down)
        value = jnp.concatenate([before, value, after], axis=dim)
    return value


def neighbour_table():
    offsets_nb = []
    for a in (-1, 0, 1):
        for b in (-1, 0, 1):
            for c in (-1, 0, 1):
                if a != 0 or b != 0 or c != 0:
                    offsets_nb.append((a, b, c, 1.0 / (a * a + b * b + c * c) ** 0.5))
    total = sum((item[3] for item in offsets_nb))
    return [(a, b, c, 4.0 * w / total) for a, b, c, w in offsets_nb]


def sweep_update(padded, average):
    depth, height, width = average.shape
    centre = padded[1 : 1 + depth, 1 : 1 + height, 1 : 1 + width]
    numerator = average
    denominator = jnp.ones_like(average)
    for a, b, c, weight_nb in neighbour_table():
        neighbour = padded[1 + a : 1 + a + depth, 1 + b : 1 + b + height, 1 + c : 1 + c + width]
        differ = centre - neighbour
        powered = jnp.power(differ * differ, 0.4)
        coefficient = weight_nb * (1.0 + QRATIO * powered) / ((1.0 + powered) * (1.0 + powered))
        numerator = numerator + coefficient * neighbour
        denominator = denominator + coefficient
    return numerator / denominator


def shards(states, footprints, offsets, measured, weights):
    current = states[0]
    blocks = footprints[:, 0]
    offsets_dev = offsets[:, 0]
    slices, height, width = current.shape
    views, foot, pixels = blocks.shape
    share = measured.shape[2]
    n_tile = lax.axis_size("tile")
    detector = share * n_tile
    n_agent = lax.axis_size("agent")
    zero_index = jnp.int32(0)
    volume = current.reshape(slices, pixels)
    projected = jnp.einsum("sp,vbp->vsb", volume, blocks, precision=lax.Precision.HIGHEST)
    partial_value = jnp.stack(
        [
            lax.dynamic_update_slice(
                jnp.zeros((slices, detector), jnp.float32),
                projected[view],
                (zero_index, offsets_dev[view]),
            )
            for view in range(views)
        ]
    )
    share_sum = lax.psum_scatter(partial_value, "tile", scatter_dimension=2, tiled=True)
    residual_share = weights * (share_sum - measured)
    residual = lax.all_gather(residual_share, "tile", axis=2, tiled=True)
    windows = jnp.stack(
        [
            lax.dynamic_slice(residual[view], (zero_index, offsets_dev[view]), (slices, foot))
            for view in range(views)
        ]
    )
    gradient = jnp.einsum("vsb,vbp->sp", windows, blocks, precision=lax.Precision.HIGHEST)
    fitted = current - STEP_SIZE * gradient.reshape(slices, height, width)
    reflect = 2.0 * fitted - current
    brick_mean = lax.psum_scatter(reflect, "agent", scatter_dimension=0, tiled=True) / n_agent
    smoothed = brick_mean
    for sweep_index in range(SWEEPS):
        padded = with_halo(smoothed, (("tile", 1), ("agent", 0)), 1)
        padded = jnp.pad(padded, ((0, 0), (0, 0), (1, 1)))
        smoothed = sweep_update(padded, brick_mean)
    prior_vol = lax.all_gather(smoothed, "agent", axis=0, tiled=True)
    current = (1.0 - RELAX) * current + RELAX * (2.0 * prior_vol - reflect)
    return (current[None], prior_vol)


def solution(mesh):
    in_specs = (
        P("agent", None, "tile", None),
        P("agent", "tile", None, None),
        P("agent", "tile"),
        P("agent", None, "tile"),
        P("agent", None, "tile"),
    )
    out_specs = (P("agent", None, "tile", None), P(None, "tile", None))
    return jax.shard_map(shards, mesh=mesh, in_specs=in_specs, out_specs=out_specs, check_vma=False)
```

profile of v0, /device:TPU:24, one launch (start us, length us, event | category | flops | bytes accessed | tf_op | source)
XLA Modules:
  0.0 878.3 jit_solution(8798802146423708650)
XLA Ops:
  7.2 1.6 fusion.17
  19.1 0.7 reshape.62
  19.8 2.6 convolution_bitcast_fusion
  30.2 4.6 copy.26
  34.8 6.5 reshape.66
  41.3 1.3 dynamic-slice.8
  42.6 444.4 %reduce-scatter.4.cloned.1.call-done = f32[32,64]{1,0:T(8,128)} async-done(((f32[2048,64]{1,0:T(8,128)}), f32[32,64]{1,0:T(8,128)}) %reduce-scatter.4.cloned.1.call-update) | async-done | bytes 8208
  487.0 0.8 reshape.67
  488.0 166.6 %all_gather.6 = f32[8,8,2048]{1,0,2:T(8,128)} all-gather(f32[8,8,32]{1,0,2:T(8,128)S(1)} %copy.12), channel_id=1, replica_groups=mesh['tile'=64,'agent'=8] {'tile'}, dimensions={2}, use_global_device_ids=true | all-gather | bytes 532480 | tf_op jit(solution)/shard_map/all_gather | solution.py:76
  654.7 29.4 %fusion.13 = (f32[1,8,2048]{1,0,2:T(1,128)}, f32[1,8,2048]{1,0,2:T(1,128)}, f32[1,8,2048]{1,0,2:T(1,128)}, f32[1,8,2048]{1,0,2:T(1,128)}, f32[1,8,2048]{1,0,2:T(...) fusion(f32[8,8,2048]{1,0,2:T(8,128)} %all_gather.6), kind=kLoop, calls=%fused_computation.61 | loop fusion | bytes 1048576 | tf_op jit(solution)/shard_map/slice | solution.py:79
  684.1 0.8 constant_dynamic-slice_fusion
  684.9 0.8 constant_dynamic-slice_fusion.2
  685.8 0.8 constant_dynamic-slice_fusion.4
  687.0 0.6 fusion.3
  687.7 65.1 %all-reduce.2 = f32[8,2,256]{2,1,0:T(2,128)S(1)} all-reduce(f32[8,2,256]{2,1,0:T(2,128)S(1)} %copy.22), channel_id=3, replica_groups=mesh['tile'=64,'agent'=8] {'agent'}, use_global_device_ids=true, to_apply=%region_1.0.clone | all-reduce | flops 4096 | bytes 32768
  752.8 0.7 dynamic-slice_multiply_fusion
  753.5 1.3 collective-permute-start
  754.8 1.3 collective-permute-start.1
  756.1 1.7 collective-permute-done.1
  757.8 15.0 %collective-permute-start.2 = (f32[1,4,256]{2,1,0:T(4,128)S(1)}, f32[1,4,256]{2,1,0:T(4,128)S(1)}, u32[]{:S(2)}, u32[]{:S(2)}) collective-permute-start(f32[1,4,256]{2,1,0:T(4,128)S(1)} %pad_maximum_fusion), channel_id=1, source_target_pairs={{0,1},{1,2},{2,3},{3,4},{4,5},{5,6},{6,7},{8,9},{9,10},{10,11},{11... | collective-permute-start | bytes 12296 | tf_op jit(solution)/shard_map/ppermute | solution.py:19
  772.8 1.9 collective-permute-start.3
  774.8 14.4 %collective-permute-done.3 = f32[1,4,256]{2,1,0:T(4,128)S(1)} collective-permute-done((f32[1,4,256]{2,1,0:T(4,128)S(1)}, f32[1,4,256]{2,1,0:T(4,128)S(1)}, u32[]{:S(2)}, u32[]{:S(2)}) %collective-permute-start.3) | collective-permute-done | bytes 4128 | tf_op jit(solution)/shard_map/ppermute | solution.py:20
  789.5 1.3 collective-permute-start.4
  790.8 1.3 collective-permute-start.5
  792.1 1.7 collective-permute-done.5
  793.9 1.9 collective-permute-start.6
  795.8 3.9 collective-permute-start.7
  799.7 12.4 %collective-permute-done.7 = f32[1,4,256]{2,1,0:T(4,128)S(1)} collective-permute-done((f32[1,4,256]{2,1,0:T(4,128)S(1)}, f32[1,4,256]{2,1,0:T(4,128)S(1)}, u32[]{:S(2)}, u32[]{:S(2)}) %collective-permute-start.7) | collective-permute-done | bytes 4128 | tf_op jit(solution)/shard_map/ppermute | solution.py:20
  812.2 0.9 add_divide_fusion
  813.1 57.1 %all_gather.7 = f32[8,2,256]{2,1,0:T(2,128)S(1)} all-gather(f32[1,2,256]{2,1,0:T(2,128)S(1)} %add_divide_fusion), channel_id=1, replica_groups=mesh['tile'=64,'agent'=8] {'agent'}, dimensions={0}, use_global_device_ids=true | all-gather | bytes 18432 | tf_op jit(solution)/shard_map/all_gather | solution.py:92
  870.2 0.6 copy.24
  870.8 0.6 copy.81
  (68 shorter events, 3.8 us)
Async XLA Ops:
  7.2 479.8 %reduce-scatter.4.cloned.1.call-start = ((), (), s32[]{:S(2)}) async-start(), calls=%async_computation.1 | async-start | bytes 1064960
  30.2 457.7 %copy-start.2 = (f32[8,8,32]{2,1,0:T(8,128)S(1)}, f32[8,8,32]{2,1,0:T(8,128)}, u32[]{:S(2)}) copy-start(f32[8,8,32]{2,1,0:T(8,128)} %param.9) | copy-start | bytes 24580
  30.2 457.7 %copy-start.3 = (f32[8,8,32]{2,1,0:T(8,128)S(1)}, f32[8,8,32]{2,1,0:T(8,128)}, u32[]{:S(2)}) copy-start(f32[8,8,32]{2,1,0:T(8,128)} %param.8) | copy-start | bytes 24580
  654.7 32.4 %copy-start = (f32[8,1,64,512]{3,2,1,0:T(8,128)S(1)}, f32[8,1,64,512]{3,2,1,0:T(8,128)}, u32[]{:S(2)}) copy-start(f32[8,1,64,512]{3,2,1,0:T(8,128)} %param.6) | copy-start | bytes 3145732
  654.7 32.4 %copy-start.1 = (f32[1,8,2,256]{3,2,1,0:T(2,128)S(1)}, f32[1,8,2,256]{3,2,1,0:T(2,128)}, u32[]{:S(2)}) copy-start(f32[1,8,2,256]{3,2,1,0:T(2,128)} %param.5) | copy-start | bytes 49156
  753.5 2.6 collective-permute-start
  754.8 3.1 collective-permute-start.1
  757.8 16.9 %collective-permute-start.2 = (f32[1,4,256]{2,1,0:T(4,128)S(1)}, f32[1,4,256]{2,1,0:T(4,128)S(1)}, u32[]{:S(2)}, u32[]{:S(2)}) collective-permute-start(f32[1,4,256]{2,1,0:T(4,128)S(1)} %pad_maximum_fusion), channel_id=1, source_target_pairs={{0,1},{1,2},{2,3},{3,4},{4,5},{5,6},{6,7},{8,9},{9,10},{10,11},{11... | collective-permute-start | bytes 12296 | tf_op jit(solution)/shard_map/ppermute | solution.py:19
  772.8 16.3 %collective-permute-start.3 = (f32[1,4,256]{2,1,0:T(4,128)S(1)}, f32[1,4,256]{2,1,0:T(4,128)S(1)}, u32[]{:S(2)}, u32[]{:S(2)}) collective-permute-start(f32[1,4,256]{2,1,0:T(4,128)S(1)} %pad_maximum_fusion), channel_id=1, source_target_pairs={{1,0},{2,1},{3,2},{4,3},{5,4},{6,5},{7,6},{9,8},{10,9},{11,10},{12... | collective-permute-start | bytes 12296 | tf_op jit(solution)/shard_map/ppermute | solution.py:20
  789.5 2.6 collective-permute-start.4
  790.8 3.1 collective-permute-start.5
  793.9 5.9 collective-permute-start.6
  795.8 16.3 %collective-permute-start.7 = (f32[1,4,256]{2,1,0:T(4,128)S(1)}, f32[1,4,256]{2,1,0:T(4,128)S(1)}, u32[]{:S(2)}, u32[]{:S(2)}) collective-permute-start(f32[1,4,256]{2,1,0:T(4,128)S(1)} %pad_maximum_fusion.1), channel_id=1, source_target_pairs={{1,0},{2,1},{3,2},{4,3},{5,4},{6,5},{7,6},{9,8},{10,9},{11,10},{12... | collective-permute-start | bytes 12296 | tf_op jit(solution)/shard_map/ppermute | solution.py:20
Sparse Core Ops, SparseCore 0:
  41.4 445.4 reduce-scatter.3
where the time goes:
time: 879 us; the launch traced here: 878 us
  waiting for transfers between devices  475 us (54%)
  blocking collectives  289 us (33%)
  local copies, waits for them, and re-layouts  51.8 us (6%)
  between operations  29.8 us (3%)
  starting transfers between devices  28 us (3%)
    unnamed x2, waiting for transfers between devices  444 us
    all_gather x1, blocking collectives, shards(): residual = lax.all_gather(residual_share, 'tile', axis=2, tiled=True)  167 us
    unnamed x1, blocking collectives  65.1 us
    all_gather x1, blocking collectives, shards(): prior_vol = lax.all_gather(smoothed, 'agent', axis=0, tiled=True)  57.1 us
    ppermute x4, waiting for transfers between devices, with_halo(): after = lax.ppermute(first, axis, down)  30.3 us
    slice x1, local copies, waits for them, and re-layouts, shards(): residual[view]  29.4 us
    ppermute x4, starting transfers between devices, with_halo(): before = lax.ppermute(last, axis, up)  19.5 us
  transfers between devices with their start and end apart: 9, of which 5 were waited for; matrix products, arithmetic and copies ran while one was open for 0% of the time, Pallas kernels for 0%

commit v1 on v0

--- a/solution.py
+++ b/solution.py
@@ -73,7 +73,9 @@
     )
     share_sum = lax.psum_scatter(partial_value, "tile", scatter_dimension=2, tiled=True)
     residual_share = weights * (share_sum - measured)
-    residual = lax.all_gather(residual_share, "tile", axis=2, tiled=True)
+    residual = jnp.concatenate(
+        lax.all_to_all(jnp.stack([residual_share] * lax.axis_size("tile")), "tile", 0, 0), axis=2
+    )
     windows = jnp.stack(
         [
             lax.dynamic_slice(residual[view], (zero_index, offsets_dev[view]), (slices, foot))

time: 879 us -> 743 us (0.85)
  the two profiles are of different devices: /device:TPU:24 before, /device:TPU:30 now
where the time goes in v1:
time: 743 us; the launch traced here: 742 us
  waiting for transfers between devices  462 us (62%)
  blocking collectives  122 us (16%)
  starting transfers between devices  93.3 us (13%)
  between operations  29.4 us (4%)
  local copies, waits for them, and re-layouts  27.5 us (4%)
    unnamed x2, waiting for transfers between devices  406 us
    unnamed x1, blocking collectives  65.2 us
    all_gather x1, blocking collectives, shards(): prior_vol = lax.all_gather(smoothed, 'agent', axis=0, tiled=True)  57.1 us
    all_to_all x1, starting transfers between devices, shards(): lax.all_to_all(jnp.stack([residual_share] * lax.axis_size('tile')), 'tile...  44.4 us
    ppermute x4, waiting for transfers between devices, with_halo(): after = lax.ppermute(first, axis, down)  29.3 us
    ppermute x4, starting transfers between devices, with_halo(): after = lax.ppermute(first, axis, down)  28.1 us
    all_to_all x1, waiting for transfers between devices, shards(): lax.all_to_all(jnp.stack([residual_share] * lax.axis_size('tile')), 'tile...  27.2 us
    ppermute x4, starting transfers between devices, with_halo(): before = lax.ppermute(last, axis, up)  20.7 us
  transfers between devices with their start and end apart: 10, of which 6 were waited for; matrix products, arithmetic and copies ran while one was open for 0% of the time, Pallas kernels for 0%

profile of v1, /device:TPU:30, one launch (start us, length us, event | category | flops | bytes accessed | tf_op | source)
XLA Modules:
  0.0 741.9 jit_solution(16554041671375853828)
XLA Ops:
  7.2 1.6 fusion.17
  18.8 0.7 reshape.69
  19.5 2.6 convolution_bitcast_fusion
  29.8 4.6 copy.29
  34.4 6.5 reshape.73
  40.9 405.9 %reduce-scatter.4.cloned.1.call-done = f32[32,64]{1,0:T(8,128)} async-done(((f32[2048,64]{1,0:T(8,128)}), f32[32,64]{1,0:T(8,128)}) %reduce-scatter.4.cloned.1.call-update) | async-done | bytes 8208
  446.7 0.8 reshape.74
  447.9 1.7 reshape.76
  449.6 44.4 %all-to-all-start = ((f32[64,1,2048]{2,1,0:T(1,128)}), f32[64,1,2048]{2,1,0:T(1,128)S(1)}, u32[]{:S(2)}, u32[]{:S(2)}) async-start(f32[64,1,2048]{2,1,0:T(1,128)} %reshape.76), calls=%async_computation | async-start | bytes 1048576 | tf_op jit(solution)/shard_map/all_to_all | solution.py:77
  494.0 1.3 dynamic-slice
  495.3 27.2 %all-to-all-done = f32[64,1,2048]{2,1,0:T(1,128)S(1)} async-done(((f32[64,1,2048]{2,1,0:T(1,128)}), f32[64,1,2048]{2,1,0:T(1,128)S(1)}, u32[]{:S(2)}, u32[]{:S(2)}) %all-to-all-start) | async-done | bytes 524320 | tf_op jit(solution)/shard_map/all_to_all | solution.py:77
  523.0 1.9 reduce
  524.9 0.7 reshape.77
  525.5 0.9 fusion.13
  526.8 1.0 copy.17
  527.9 1.0 copy.18
  531.2 65.2 %all-reduce.2 = f32[8,2,256]{2,1,0:T(2,128)S(1)} all-reduce(f32[8,2,256]{2,1,0:T(2,128)S(1)} %copy.25), channel_id=3, replica_groups=mesh['tile'=64,'agent'=8] {'agent'}, use_global_device_ids=true, to_apply=%region_1.0.clone | all-reduce | flops 4096 | bytes 32768
  596.4 0.7 dynamic-slice_multiply_fusion
  597.1 1.9 collective-permute-start
  599.0 11.1 %collective-permute-start.1 = (f32[1,1,256]{2,1,0:T(1,128)S(1)}, f32[1,1,256]{2,1,0:T(1,128)S(1)}, u32[]{:S(2)}, u32[]{:S(2)}) collective-permute-start(f32[1,1,256]{2,1,0:T(1,128)S(1)} %get-tuple-element.27), channel_id=1, source_target_pairs={{8,0},{16,8},{24,16},{32,24},{40,32},{48,40},{56,48},{64,56},{72,6... | collective-permute-start | bytes 3080 | tf_op jit(solution)/shard_map/ppermute | solution.py:20
  610.2 1.3 collective-permute-done.1
  611.4 15.0 %collective-permute-start.2 = (f32[1,4,256]{2,1,0:T(4,128)S(1)}, f32[1,4,256]{2,1,0:T(4,128)S(1)}, u32[]{:S(2)}, u32[]{:S(2)}) collective-permute-start(f32[1,4,256]{2,1,0:T(4,128)S(1)} %pad_maximum_fusion), channel_id=1, source_target_pairs={{0,1},{1,2},{2,3},{3,4},{4,5},{5,6},{6,7},{8,9},{9,10},{10,11},{11... | collective-permute-start | bytes 12296 | tf_op jit(solution)/shard_map/ppermute | solution.py:19
  626.5 1.9 collective-permute-start.3
  628.4 14.4 %collective-permute-done.3 = f32[1,4,256]{2,1,0:T(4,128)S(1)} collective-permute-done((f32[1,4,256]{2,1,0:T(4,128)S(1)}, f32[1,4,256]{2,1,0:T(4,128)S(1)}, u32[]{:S(2)}, u32[]{:S(2)}) %collective-permute-start.3) | collective-permute-done | bytes 4128 | tf_op jit(solution)/shard_map/ppermute | solution.py:20
  643.1 1.9 collective-permute-start.4
  645.0 11.1 %collective-permute-start.5 = (f32[1,1,256]{2,1,0:T(1,128)S(1)}, f32[1,1,256]{2,1,0:T(1,128)S(1)}, u32[]{:S(2)}, u32[]{:S(2)}) collective-permute-start(f32[1,1,256]{2,1,0:T(1,128)S(1)} %get-tuple-element.25), channel_id=1, source_target_pairs={{8,0},{16,8},{24,16},{32,24},{40,32},{48,40},{56,48},{64,56},{72,6... | collective-permute-start | bytes 3080 | tf_op jit(solution)/shard_map/ppermute | solution.py:20
  656.2 1.3 collective-permute-done.5
  657.5 1.9 collective-permute-start.6
  659.4 3.9 collective-permute-start.7
  663.3 12.4 %collective-permute-done.7 = f32[1,4,256]{2,1,0:T(4,128)S(1)} collective-permute-done((f32[1,4,256]{2,1,0:T(4,128)S(1)}, f32[1,4,256]{2,1,0:T(4,128)S(1)}, u32[]{:S(2)}, u32[]{:S(2)}) %collective-permute-start.7) | collective-permute-done | bytes 4128 | tf_op jit(solution)/shard_map/ppermute | solution.py:20
  675.8 0.9 add_divide_fusion
  676.7 57.1 %all_gather.3 = f32[8,2,256]{2,1,0:T(2,128)S(1)} all-gather(f32[1,2,256]{2,1,0:T(2,128)S(1)} %add_divide_fusion), channel_id=1, replica_groups=mesh['tile'=64,'agent'=8] {'agent'}, dimensions={0}, use_global_device_ids=true | all-gather | bytes 18432 | tf_op jit(solution)/shard_map/all_gather | solution.py:94
  (77 shorter events, 7.8 us)
Async XLA Ops:
  7.2 439.6 %reduce-scatter.4.cloned.1.call-start = ((), (), s32[]{:S(2)}) async-start(), calls=%async_computation.2 | async-start | bytes 1064960
  34.4 413.3 %copy-start.2 = (f32[8,8,32]{2,1,0:T(8,128)S(1)}, f32[8,8,32]{2,1,0:T(8,128)}, u32[]{:S(2)}) copy-start(f32[8,8,32]{2,1,0:T(8,128)} %param.9) | copy-start | bytes 24580
  34.4 413.3 %copy-start.3 = (f32[8,8,32]{2,1,0:T(8,128)S(1)}, f32[8,8,32]{2,1,0:T(8,128)}, u32[]{:S(2)}) copy-start(f32[8,8,32]{2,1,0:T(8,128)} %param.8) | copy-start | bytes 24580
  449.6 72.8 %all-to-all-start = ((f32[64,1,2048]{2,1,0:T(1,128)}), f32[64,1,2048]{2,1,0:T(1,128)S(1)}, u32[]{:S(2)}, u32[]{:S(2)}) async-start(f32[64,1,2048]{2,1,0:T(1,128)} %reshape.76), calls=%async_computation | async-start | bytes 1048576 | tf_op jit(solution)/shard_map/all_to_all | solution.py:77
  529.1 1.5 copy-start
  529.1 1.5 copy-start.1
  597.1 13.1 %collective-permute-start = (f32[1,1,256]{2,1,0:T(1,128)S(1)}, f32[1,1,256]{2,1,0:T(1,128)S(1)}, u32[]{:S(2)}, u32[]{:S(2)}) collective-permute-start(f32[1,1,256]{2,1,0:T(1,128)S(1)} %get-tuple-element.26), channel_id=1, source_target_pairs={{0,8},{8,16},{16,24},{24,32},{32,40},{40,48},{48,56},{56,64},{64,7... | collective-permute-start | bytes 3080 | tf_op jit(solution)/shard_map/ppermute | solution.py:19
  599.0 12.4 %collective-permute-start.1 = (f32[1,1,256]{2,1,0:T(1,128)S(1)}, f32[1,1,256]{2,1,0:T(1,128)S(1)}, u32[]{:S(2)}, u32[]{:S(2)}) collective-permute-start(f32[1,1,256]{2,1,0:T(1,128)S(1)} %get-tuple-element.27), channel_id=1, source_target_pairs={{8,0},{16,8},{24,16},{32,24},{40,32},{48,40},{56,48},{64,56},{72,6... | collective-permute-start | bytes 3080 | tf_op jit(solution)/shard_map/ppermute | solution.py:20
  611.4 16.9 %collective-permute-start.2 = (f32[1,4,256]{2,1,0:T(4,128)S(1)}, f32[1,4,256]{2,1,0:T(4,128)S(1)}, u32[]{:S(2)}, u32[]{:S(2)}) collective-permute-start(f32[1,4,256]{2,1,0:T(4,128)S(1)} %pad_maximum_fusion), channel_id=1, source_target_pairs={{0,1},{1,2},{2,3},{3,4},{4,5},{5,6},{6,7},{8,9},{9,10},{10,11},{11... | collective-permute-start | bytes 12296 | tf_op jit(solution)/shard_map/ppermute | solution.py:19
  626.5 16.3 %collective-permute-start.3 = (f32[1,4,256]{2,1,0:T(4,128)S(1)}, f32[1,4,256]{2,1,0:T(4,128)S(1)}, u32[]{:S(2)}, u32[]{:S(2)}) collective-permute-start(f32[1,4,256]{2,1,0:T(4,128)S(1)} %pad_maximum_fusion), channel_id=1, source_target_pairs={{1,0},{2,1},{3,2},{4,3},{5,4},{6,5},{7,6},{9,8},{10,9},{11,10},{12... | collective-permute-start | bytes 12296 | tf_op jit(solution)/shard_map/ppermute | solution.py:20
  643.1 13.1 %collective-permute-start.4 = (f32[1,1,256]{2,1,0:T(1,128)S(1)}, f32[1,1,256]{2,1,0:T(1,128)S(1)}, u32[]{:S(2)}, u32[]{:S(2)}) collective-permute-start(f32[1,1,256]{2,1,0:T(1,128)S(1)} %get-tuple-element.24), channel_id=1, source_target_pairs={{0,8},{8,16},{16,24},{24,32},{32,40},{40,48},{48,56},{56,64},{64,7... | collective-permute-start | bytes 3080 | tf_op jit(solution)/shard_map/ppermute | solution.py:19
  645.0 12.4 %collective-permute-start.5 = (f32[1,1,256]{2,1,0:T(1,128)S(1)}, f32[1,1,256]{2,1,0:T(1,128)S(1)}, u32[]{:S(2)}, u32[]{:S(2)}) collective-permute-start(f32[1,1,256]{2,1,0:T(1,128)S(1)} %get-tuple-element.25), channel_id=1, source_target_pairs={{8,0},{16,8},{24,16},{32,24},{40,32},{48,40},{56,48},{64,56},{72,6... | collective-permute-start | bytes 3080 | tf_op jit(solution)/shard_map/ppermute | solution.py:20
  657.5 5.8 collective-permute-start.6
  659.4 16.3 %collective-permute-start.7 = (f32[1,4,256]{2,1,0:T(4,128)S(1)}, f32[1,4,256]{2,1,0:T(4,128)S(1)}, u32[]{:S(2)}, u32[]{:S(2)}) collective-permute-start(f32[1,4,256]{2,1,0:T(4,128)S(1)} %pad_maximum_fusion.1), channel_id=1, source_target_pairs={{1,0},{2,1},{3,2},{4,3},{5,4},{6,5},{7,6},{9,8},{10,9},{11,10},{12... | collective-permute-start | bytes 12296 | tf_op jit(solution)/shard_map/ppermute | solution.py:20
Sparse Core Ops, SparseCore 0:
  41.0 405.6 reduce-scatter.3
